TPU v7x, 256 devices: a whole 4x4x8 slice. The times are simulated.
256 devices in a mesh: row: 16 (over y, x), col: 16 (over z, core).
Axes of the slice: x: 4, y: 4, z: 8, core: 2. Of those that a mesh axis runs over, the one named last changes fastest.
Arguments:
- rhs: float32 [128, 32768], P('row', 'col'), may hold values from -60 to 60
- flex_tiles: float32 [131072, 2048], P('row', 'col'), may hold values from -0.25 to 0.25
- flex_cols: int32 [256, 64], P('row', 'col'), may hold values from 0 to 15, as said below
- stiff_tiles: float32 [131072, 2048], P('row', 'col'), may hold values from -0.25 to 0.25
- stiff_cols: int32 [256, 64], P('row', 'col'), may hold values from 0 to 15, as said below
- deflation: float32 [512, 32768], P('row', 'col'), may hold values from -0.375 to 0.375
- coarse_rows: float32 [8192, 8192], P(('row', 'col')), may hold values from -5 to 5, as said below
- face_rows: int32 [64, 2048], P('row', 'col'), may hold values from 0 to 2047, as said below
- face_len: int32 [16, 64], P('row', 'col'), may hold values from 0 to 128, as said below
Outputs:
- solution: float32 [128, 32768], P('row', 'col')
- residual: float32 [128, 32768], P('row', 'col')
- correction: float32 [128, 32768], P('row', 'col')
Inputs may be any that keep to these rules, and one draw needn't show every extreme that they name: `flex_cols`: row b of a subdomain's block list names 4 different block columns, the first being b. `stiff_cols`: row b of a subdomain's block list names 4 different block columns, the first being b. `coarse_rows`: the whole matrix is symmetric. `face_rows`: the four lists of a subdomain name 512 different multipliers of it. `face_len`: the two subdomains of a face give it the same length; faces on the grid's boundary have length 0, inner faces at least 32.
All inputs are finite; a program needn't handle non-finite values.
Results may differ from a plain program's by a relative error of at most 0.0003.
Values sent between devices are 32-bit elements; how exact they have to be, the bound alone decides.
A program may use at most 64 MiB of HBM per device.

v0:
```python
import jax
import jax.numpy as jnp
from jax import lax
from jax.sharding import PartitionSpec as P

ITERS = 3
PRECISE = lax.Precision.HIGHEST


def with_halo(cells, sides, width):
    for axis, dim in sides:
        count = lax.axis_size(axis)
        ends = count - 1
        head = lax.slice_in_dim(cells, 0, width, axis=dim)
        tail = lax.slice_in_dim(cells, cells.shape[dim] - width, cells.shape[dim], axis=dim)
        cells = jnp.concatenate(
            [
                lax.ppermute(tail, axis, [(i, (i + 1) % count) for i in range(ends)]),
                cells,
                lax.ppermute(head, axis, [((i + 1) % count, i) for i in range(ends)]),
            ],
            axis=dim,
        )
    return cells


def sparse_forward(vector, tile_set, columns):
    load_count = vector.shape[0]
    blocks, per_row = columns.shape
    tile_width = tile_set.shape[-1]
    pieces = vector.reshape(load_count, blocks, tile_width)
    picked = jnp.take(pieces, columns.reshape(-1), axis=1).reshape(
        load_count, blocks, per_row, tile_width
    )
    product = jnp.einsum("lbkw,bkwv->lbv", picked, tile_set, precision=PRECISE)
    return product.reshape(load_count, blocks * tile_width)


def sparse_backward(vector, tile_set, columns):
    load_count = vector.shape[0]
    blocks, per_row = columns.shape
    tile_width = tile_set.shape[-1]
    pieces = vector.reshape(load_count, blocks, tile_width)
    product = jnp.einsum("lbv,bkwv->lbkw", pieces, tile_set, precision=PRECISE)
    onehot = (columns[:, :, None] == jnp.arange(blocks, dtype=jnp.int32)[None, None, :]).astype(
        jnp.float32
    )
    summed = jnp.einsum("lbkw,bkj->ljw", product, onehot, precision=PRECISE)
    return summed.reshape(load_count, blocks * tile_width)


def pair_totals(first_field, second_field, third_field, fourth_field):
    return lax.psum(
        (jnp.sum(first_field * second_field, axis=1), jnp.sum(third_field * fourth_field, axis=1)),
        ("row", "col"),
    )


def shards(
    rhs, flex_tiles, flex_cols, stiff_tiles, stiff_cols, deflation, coarse_rows, face_rows, face_len
):
    blocks, per_row = flex_cols.shape
    tile_width = flex_tiles.shape[1]
    flex_set = flex_tiles.reshape(blocks, per_row, tile_width, tile_width)
    stiff_set = stiff_tiles.reshape(blocks, per_row, tile_width, tile_width)
    face_width = face_rows.shape[1]
    flat_index = face_rows.reshape(-1)
    slots = jnp.arange(face_width, dtype=jnp.int32)
    live_mask = (slots[None, :] < face_len.reshape(4, 1)).astype(jnp.float32)

    def face_part(vector):
        load_count = vector.shape[0]
        traces = jnp.take(vector, flat_index, axis=1).reshape(load_count, 4, face_width)
        across_rows = with_halo(traces[:, 0:2], (("row", 1),), 1)
        across_cols = with_halo(traces[:, 2:4], (("col", 1),), 1)
        partner = jnp.stack(
            [across_rows[:, 0], across_rows[:, 3], across_cols[:, 0], across_cols[:, 3]], axis=1
        )
        jump_values = (traces - partner) * live_mask[None]
        return (
            jnp.zeros_like(vector)
            .at[:, flat_index]
            .add(jump_values.reshape(load_count, 4 * face_width))
        )

    def operate(vector):
        coupling = face_part(vector)
        after_flex = sparse_forward(vector, flex_set, flex_cols)
        after_stiff = sparse_forward(after_flex, stiff_set, stiff_cols)
        back_stiff = sparse_backward(after_stiff, stiff_set, stiff_cols)
        local_part = sparse_backward(back_stiff, flex_set, flex_cols)
        return vector + local_part + coupling

    def precondition(vector):
        coefficients = jnp.einsum("lm,dm->ld", vector, deflation, precision=PRECISE)
        energy = jnp.einsum(
            "ln,dn->ld",
            lax.all_gather(coefficients, ("row", "col"), axis=1, tiled=True),
            coarse_rows,
            precision=PRECISE,
        )
        return vector + jnp.einsum("ld,dm->lm", energy, deflation, precision=PRECISE)

    residual = rhs
    solution = jnp.zeros_like(rhs)
    correction = precondition(residual)
    direction = correction
    image = operate(direction)
    curvature_sum, descent_sum = pair_totals(direction, image, residual, direction)
    for iteration in range(ITERS):
        step_size = (descent_sum / curvature_sum)[:, None]
        solution = solution + step_size * direction
        residual = residual - step_size * image
        correction = precondition(residual)
        if iteration + 1 < ITERS:
            cross_sum = lax.psum(jnp.sum(correction * image, axis=1), ("row", "col"))
            blend = -cross_sum / curvature_sum
            direction = correction + blend[:, None] * direction
            image = operate(direction)
            curvature_sum, descent_sum = pair_totals(direction, image, residual, direction)
    return (solution, residual, correction)


def solution(mesh):
    return jax.shard_map(
        shards,
        mesh=mesh,
        in_specs=(
            P("row", "col"),
            P("row", "col"),
            P("row", "col"),
            P("row", "col"),
            P("row", "col"),
            P("row", "col"),
            P(("row", "col"), None),
            P("row", "col"),
            P("row", "col"),
        ),
        out_specs=(P("row", "col"), P("row", "col"), P("row", "col")),
        check_vma=False,
    )
```

profile of v0, /device:TPU:1, one launch (start us, length us, event | category | flops | bytes accessed | tf_op | source)
XLA Modules:
  0.0 747.8 jit_solution(5366016694959184341)
XLA Ops:
  0.7 0.8 compare_select_fusion.1
  1.5 0.7 compare_and_fusion
  2.1 1.2 convolution_bitcast_fusion.21
  3.4 67.8 %all-gather = f32[256,32,8]{1,2,0:T(8,128)S(1)} all-gather(f32[1,32,8]{1,2,0:T(8,128)S(1)} %convolution_bitcast_fusion.21), channel_id=1, replica_groups=mesh['row'=16,'col'=16] {'row','col'}, dimensions={0}, use_global_device_ids=true | all-gather | bytes 263168 | tf_op jit(solution)/shard_map/all_gather | solution.py:98
  71.9 0.9 fusion.36
  73.5 1.0 gather_fusion.2
  74.7 2.6 collective-permute-start
  77.4 1.3 collective-permute-start.1
  78.8 1.9 collective-permute-start.2
  80.8 2.7 collective-permute-start.3
  84.8 3.8 convolution_bitcast_fusion.17
  89.4 4.0 convolution_bitcast_fusion.16
  93.5 3.6 convolution_bitcast_fusion.5
  97.4 3.6 convolution_bitcast_fusion.4
  102.2 4.2 scatter_custom_fusion
  106.9 78.0 %all-reduce.2 = (f32[8]{0:T(128)S(1)}, f32[8]{0:T(128)S(1)}) all-reduce(f32[8]{0:T(128)S(1)} %get-tuple-element.10, f32[8]{0:T(128)S(1)} %get-tuple-element.9), channel_id=1, replica_groups=mesh['row'=16,'col'=16] {'row','col'}, use_global_device_ids=true, to_apply=%region_1.2 | all-reduce | flops 16 | bytes 128 | tf_op jit(solution)/shard_map/psum | solution.py:53
  185.2 60.6 %all-gather.1 = f32[256,32,8]{1,2,0:T(8,128)S(1)} all-gather(f32[1,32,8]{1,2,0:T(8,128)S(1)} %convolution_bitcast_fusion.20), channel_id=1, replica_groups=mesh['row'=16,'col'=16] {'row','col'}, dimensions={0}, use_global_device_ids=true | all-gather | bytes 263168 | tf_op jit(solution)/shard_map/all_gather | solution.py:98
  246.5 0.9 fusion.37
  247.8 75.0 %psum.58 = f32[8]{0:T(128)S(1)} all-reduce(f32[8]{0:T(128)S(1)} %get-tuple-element.31), channel_id=1, replica_groups=mesh['row'=16,'col'=16] {'row','col'}, use_global_device_ids=true, to_apply=%region_6.9 | all-reduce | flops 8 | bytes 64 | tf_op jit(solution)/shard_map/psum | solution.py:116
  323.3 1.0 gather_fusion.5
  324.6 1.6 collective-permute-start.4
  326.2 1.3 collective-permute-start.5
  327.5 4.5 collective-permute-start.6
  332.1 2.1 collective-permute-start.7
  335.0 3.8 convolution_bitcast_fusion.15
  339.7 4.0 convolution_bitcast_fusion.14
  343.7 3.6 convolution_bitcast_fusion.3
  347.6 3.6 convolution_bitcast_fusion.2
  352.4 3.9 scatter_custom_fusion.1
  356.8 77.0 %all-reduce.1 = (f32[8]{0:T(128)S(1)}, f32[8]{0:T(128)S(1)}) all-reduce(f32[8]{0:T(128)S(1)} %get-tuple-element.8, f32[8]{0:T(128)S(1)} %get-tuple-element.7), channel_id=1, replica_groups=mesh['row'=16,'col'=16] {'row','col'}, use_global_device_ids=true, to_apply=%region_8.11 | all-reduce | flops 16 | bytes 128 | tf_op jit(solution)/shard_map/psum | solution.py:53
  434.1 61.9 %all-gather.2 = f32[256,32,8]{1,2,0:T(8,128)S(1)} all-gather(f32[1,32,8]{1,2,0:T(8,128)S(1)} %convolution_bitcast_fusion.19), channel_id=1, replica_groups=mesh['row'=16,'col'=16] {'row','col'}, dimensions={0}, use_global_device_ids=true | all-gather | bytes 263168 | tf_op jit(solution)/shard_map/all_gather | solution.py:98
  496.7 0.9 fusion.38
  498.0 73.7 %psum.61 = f32[8]{0:T(128)S(1)} all-reduce(f32[8]{0:T(128)S(1)} %get-tuple-element.33), channel_id=1, replica_groups=mesh['row'=16,'col'=16] {'row','col'}, use_global_device_ids=true, to_apply=%region_13.16 | all-reduce | flops 8 | bytes 64 | tf_op jit(solution)/shard_map/psum | solution.py:116
  572.1 1.0 gather_fusion.8
  573.4 3.8 collective-permute-start.10
  577.3 1.9 collective-permute-start.11
  579.2 2.0 collective-permute-start.8
  581.3 1.7 collective-permute-start.9
  583.8 3.8 convolution_bitcast_fusion.13
  588.4 4.0 convolution_bitcast_fusion.12
  592.4 3.6 convolution_bitcast_fusion.1
  596.4 3.6 convolution_bitcast_fusion
  601.1 3.9 scatter_custom_fusion.2
  605.5 77.2 %all-reduce = (f32[8]{0:T(128)S(1)}, f32[8]{0:T(128)S(1)}) all-reduce(f32[8]{0:T(128)S(1)} %get-tuple-element.6, f32[8]{0:T(128)S(1)} %get-tuple-element.5), channel_id=1, replica_groups=mesh['row'=16,'col'=16] {'row','col'}, use_global_device_ids=true, to_apply=%region_15.18 | all-reduce | flops 16 | bytes 128 | tf_op jit(solution)/shard_map/psum | solution.py:53
  682.7 0.7 multiply_subtract_fusion
  683.7 61.3 %all-gather.3 = f32[256,32,8]{1,2,0:T(8,128)S(1)} all-gather(f32[1,32,8]{1,2,0:T(8,128)S(1)} %convolution_bitcast_fusion.18), channel_id=1, replica_groups=mesh['row'=16,'col'=16] {'row','col'}, dimensions={0}, use_global_device_ids=true | all-gather | bytes 263168 | tf_op jit(solution)/shard_map/all_gather | solution.py:98
  745.8 0.9 fusion.39
  746.7 0.9 convolution_add_fusion
  (137 shorter events, 18.0 us)
Async XLA Ops:
  0.6 71.3 %copy-start = (f32[32,8192]{1,0:T(8,128)S(1)}, f32[32,8192]{1,0:T(8,128)}, u32[]{:S(2)}) copy-start(f32[32,8192]{1,0:T(8,128)} %param.19) | copy-start | bytes 3145732
  0.6 72.2 %copy-start.8 = (f32[8,2048]{1,0:T(8,128)S(1)}, f32[8,2048]{1,0:T(8,128)}, u32[]{:S(2)}) copy-start(f32[8,2048]{1,0:T(8,128)} %param.13) | copy-start | bytes 196612
  0.7 72.2 %copy-start.7 = (f32[32,2048]{1,0:T(8,128)S(1)}, f32[32,2048]{1,0:T(8,128)}, u32[]{:S(2)}) copy-start(f32[32,2048]{1,0:T(8,128)} %param.18) | copy-start | bytes 786436
  3.4 80.1 %copy-start.11 = (s32[16,4]{0,1:T(4,128)S(1)}, s32[16,4]{0,1:T(4,128)}, u32[]{:S(2)}) copy-start(s32[16,4]{0,1:T(4,128)} %param.15) | copy-start | bytes 772
  3.4 80.3 %copy-start.10 = (s32[16,4]{0,1:T(4,128)S(1)}, s32[16,4]{0,1:T(4,128)}, u32[]{:S(2)}) copy-start(s32[16,4]{0,1:T(4,128)} %param.17) | copy-start | bytes 772
  3.4 80.5 %copy-start.13 = (s32[1,4]{1,0:T(1,128)S(1)}, s32[1,4]{1,0:T(1,128)}, u32[]{:S(2)}) copy-start(s32[1,4]{1,0:T(1,128)} %param.21) | copy-start | bytes 52
  74.7 27.1 %collective-permute-start = (f32[8,1,128]{2,0,1:T(8,128)S(1)}, f32[8,1,128]{2,0,1:T(8,128)S(1)}, u32[]{:S(2)}, u32[]{:S(2)}) collective-permute-start(f32[8,1,128]{2,0,1:T(8,128)S(1)} %copy.118), channel_id=1, source_target_pairs={{0,16},{16,32},{32,48},{48,64},{64,80},{80,96},{96,112},{112,128},... | collective-permute-start | bytes 12296 | tf_op jit(solution)/shard_map/ppermute | solution.py:18
  77.4 24.4 %collective-permute-start.1 = (f32[8,1,128]{2,0,1:T(8,128)S(1)}, f32[8,1,128]{2,0,1:T(8,128)S(1)}, u32[]{:S(2)}, u32[]{:S(2)}) collective-permute-start(f32[8,1,128]{2,0,1:T(8,128)S(1)} %copy.119), channel_id=1, source_target_pairs={{16,0},{32,16},{48,32},{64,48},{80,64},{96,80},{112,96},{128,112},... | collective-permute-start | bytes 12296 | tf_op jit(solution)/shard_map/ppermute | solution.py:20
  78.8 23.0 %collective-permute-start.2 = (f32[8,1,128]{2,0,1:T(8,128)S(1)}, f32[8,1,128]{2,0,1:T(8,128)S(1)}, u32[]{:S(2)}, u32[]{:S(2)}) collective-permute-start(f32[8,1,128]{2,0,1:T(8,128)S(1)} %copy.120), channel_id=1, source_target_pairs={{0,1},{1,2},{2,3},{3,4},{4,5},{5,6},{6,7},{7,8},{8,9},{9,10},{10,1... | collective-permute-start | bytes 12296 | tf_op jit(solution)/shard_map/ppermute | solution.py:18
  80.8 21.1 %collective-permute-start.3 = (f32[8,1,128]{2,0,1:T(8,128)S(1)}, f32[8,1,128]{2,0,1:T(8,128)S(1)}, u32[]{:S(2)}, u32[]{:S(2)}) collective-permute-start(f32[8,1,128]{2,0,1:T(8,128)S(1)} %copy.121), channel_id=1, source_target_pairs={{1,0},{2,1},{3,2},{4,3},{5,4},{6,5},{7,6},{8,7},{9,8},{10,9},{11,1... | collective-permute-start | bytes 12296 | tf_op jit(solution)/shard_map/ppermute | solution.py:20
  89.3 4.2 copy-start.1
  89.4 8.0 %copy-start.4 = (f32[8192,128]{1,0:T(8,128)S(1)}, f32[8192,128]{1,0:T(8,128)}, u32[]{:S(2)}) copy-start(f32[8192,128]{1,0:T(8,128)} %param.14) | copy-start | bytes 12582916
  93.4 8.0 %copy-start.12 = (s32[4,128]{1,0:T(4,128)S(1)}, s32[4,128]{1,0:T(4,128)}, u32[]{:S(2)}) copy-start(s32[4,128]{1,0:T(4,128)} %param.20) | copy-start | bytes 6148
  324.6 27.4 %collective-permute-start.4 = (f32[8,1,128]{2,0,1:T(8,128)S(1)}, f32[8,1,128]{2,0,1:T(8,128)S(1)}, u32[]{:S(2)}, u32[]{:S(2)}) collective-permute-start(f32[8,1,128]{2,0,1:T(8,128)S(1)} %copy.122), channel_id=1, source_target_pairs={{0,16},{16,32},{32,48},{48,64},{64,80},{80,96},{96,112},{112,128},... | collective-permute-start | bytes 12296 | tf_op jit(solution)/shard_map/ppermute | solution.py:18
  326.2 25.8 %collective-permute-start.5 = (f32[8,1,128]{2,0,1:T(8,128)S(1)}, f32[8,1,128]{2,0,1:T(8,128)S(1)}, u32[]{:S(2)}, u32[]{:S(2)}) collective-permute-start(f32[8,1,128]{2,0,1:T(8,128)S(1)} %copy.123), channel_id=1, source_target_pairs={{16,0},{32,16},{48,32},{64,48},{80,64},{96,80},{112,96},{128,112},... | collective-permute-start | bytes 12296 | tf_op jit(solution)/shard_map/ppermute | solution.py:20
  327.5 24.5 %collective-permute-start.6 = (f32[8,1,128]{2,0,1:T(8,128)S(1)}, f32[8,1,128]{2,0,1:T(8,128)S(1)}, u32[]{:S(2)}, u32[]{:S(2)}) collective-permute-start(f32[8,1,128]{2,0,1:T(8,128)S(1)} %copy.124), channel_id=1, source_target_pairs={{0,1},{1,2},{2,3},{3,4},{4,5},{5,6},{6,7},{7,8},{8,9},{9,10},{10,1... | collective-permute-start | bytes 12296 | tf_op jit(solution)/shard_map/ppermute | solution.py:18
  332.1 19.9 %collective-permute-start.7 = (f32[8,1,128]{2,0,1:T(8,128)S(1)}, f32[8,1,128]{2,0,1:T(8,128)S(1)}, u32[]{:S(2)}, u32[]{:S(2)}) collective-permute-start(f32[8,1,128]{2,0,1:T(8,128)S(1)} %copy.125), channel_id=1, source_target_pairs={{1,0},{2,1},{3,2},{4,3},{5,4},{6,5},{7,6},{8,7},{9,8},{10,9},{11,1... | collective-permute-start | bytes 12296 | tf_op jit(solution)/shard_map/ppermute | solution.py:20
  339.5 4.2 copy-start.2
  339.6 8.0 %copy-start.5 = (f32[8192,128]{1,0:T(8,128)S(1)}, f32[8192,128]{1,0:T(8,128)}, u32[]{:S(2)}) copy-start(f32[8192,128]{1,0:T(8,128)} %param.14) | copy-start | bytes 12582916
  573.4 27.4 %collective-permute-start.10 = (f32[8,1,128]{2,0,1:T(8,128)S(1)}, f32[8,1,128]{2,0,1:T(8,128)S(1)}, u32[]{:S(2)}, u32[]{:S(2)}) collective-permute-start(f32[8,1,128]{2,0,1:T(8,128)S(1)} %copy.128), channel_id=1, source_target_pairs={{0,1},{1,2},{2,3},{3,4},{4,5},{5,6},{6,7},{7,8},{8,9},{9,10},{10,1... | collective-permute-start | bytes 12296 | tf_op jit(solution)/shard_map/ppermute | solution.py:18
  577.3 23.5 %collective-permute-start.11 = (f32[8,1,128]{2,0,1:T(8,128)S(1)}, f32[8,1,128]{2,0,1:T(8,128)S(1)}, u32[]{:S(2)}, u32[]{:S(2)}) collective-permute-start(f32[8,1,128]{2,0,1:T(8,128)S(1)} %copy.129), channel_id=1, source_target_pairs={{1,0},{2,1},{3,2},{4,3},{5,4},{6,5},{7,6},{8,7},{9,8},{10,9},{11,1... | collective-permute-start | bytes 12296 | tf_op jit(solution)/shard_map/ppermute | solution.py:20
  579.2 21.5 %collective-permute-start.8 = (f32[8,1,128]{2,0,1:T(8,128)S(1)}, f32[8,1,128]{2,0,1:T(8,128)S(1)}, u32[]{:S(2)}, u32[]{:S(2)}) collective-permute-start(f32[8,1,128]{2,0,1:T(8,128)S(1)} %copy.126), channel_id=1, source_target_pairs={{0,16},{16,32},{32,48},{48,64},{64,80},{80,96},{96,112},{112,128},... | collective-permute-start | bytes 12296 | tf_op jit(solution)/shard_map/ppermute | solution.py:18
  581.3 19.5 %collective-permute-start.9 = (f32[8,1,128]{2,0,1:T(8,128)S(1)}, f32[8,1,128]{2,0,1:T(8,128)S(1)}, u32[]{:S(2)}, u32[]{:S(2)}) collective-permute-start(f32[8,1,128]{2,0,1:T(8,128)S(1)} %copy.127), channel_id=1, source_target_pairs={{16,0},{32,16},{48,32},{64,48},{80,64},{96,80},{112,96},{128,112},... | collective-permute-start | bytes 12296 | tf_op jit(solution)/shard_map/ppermute | solution.py:20
  588.2 4.2 copy-start.3
  588.4 8.0 %copy-start.6 = (f32[8192,128]{1,0:T(8,128)S(1)}, f32[8192,128]{1,0:T(8,128)}, u32[]{:S(2)}) copy-start(f32[8192,128]{1,0:T(8,128)} %param.14) | copy-start | bytes 12582916
  683.5 64.1 %copy-start.9 = (f32[8,2048]{1,0:T(8,128)}, f32[8,2048]{1,0:T(8,128)S(1)}, u32[]{:S(2)}) copy-start(f32[8,2048]{1,0:T(8,128)S(1)} %get-tuple-element.29) | copy-start | bytes 196612
where the time goes:
time: 753 us; the launch traced here: 748 us
  blocking collectives  633 us (84%)
  matrix products  54.8 us (7%)
  starting transfers between devices  27.5 us (4%)
  other arithmetic  17 us (2%)
  local copies, waits for them, and re-layouts  14.1 us (2%)
    all_gather x4, blocking collectives, precondition(): lax.all_gather(coefficients, ('row', 'col'), axis=1, tiled=True)  252 us
    psum x3, blocking collectives, pair_totals(): lax.psum((jnp.sum(first_field * second_field, axis=1), jnp.sum(third_fiel...  232 us
    psum x2, blocking collectives, shards(): cross_sum = lax.psum(jnp.sum(correction * image, axis=1), ('row', 'col'))  149 us
    dot_general x6, matrix products, sparse_forward(): product = jnp.einsum('lbkw,bkwv->lbv', picked, tile_set, precision=PRECISE)  23.5 us
    dot_general x6, matrix products, sparse_backward(): product = jnp.einsum('lbv,bkwv->lbkw', pieces, tile_set, precision=PRECISE)  21.4 us
    ppermute x6, starting transfers between devices, with_halo(): lax.ppermute(tail, axis, [(i, (i + 1) % count) for i in range(ends)])  16.4 us
  transfers between devices with their start and end apart: 12, of which 0 were waited for; matrix products, arithmetic and copies ran while one was open for 7% of the time, Pallas kernels for 0%

commit v1 on v0

--- a/solution.py
+++ b/solution.py
@@ -95,7 +95,12 @@
         coefficients = jnp.einsum("lm,dm->ld", vector, deflation, precision=PRECISE)
         energy = jnp.einsum(
             "ln,dn->ld",
-            lax.all_gather(coefficients, ("row", "col"), axis=1, tiled=True),
+            jnp.concatenate(
+                lax.all_to_all(
+                    jnp.stack([coefficients] * lax.axis_size(("row", "col"))), ("row", "col"), 0, 0
+                ),
+                axis=1,
+            ),
             coarse_rows,
             precision=PRECISE,
         )

time: 753 us -> 617 us (0.82)
  blocking collectives: 633 us -> 444 us
  starting transfers between devices: 27.5 us -> 45 us
  other arithmetic: 17 us -> 29.2 us
  waiting for transfers between devices: 0.03 us -> 11.3 us
  local copies, waits for them, and re-layouts: 14.1 us -> 22.8 us
    all_gather x4 -> x0, blocking collectives: 252 us -> none  [precondition(): lax.all_gather(coefficients, ('row', 'col'), axis=1, tiled=True)]
    all_to_all x0 -> x3, blocking collectives: none -> 68 us  [precondition(): lax.all_to_all(jnp.stack([coefficients] * lax.axis_size(('row', 'col'))),...]
    all_to_all x0 -> x1, starting transfers between devices: none -> 15.6 us  [precondition(): lax.all_to_all(jnp.stack([coefficients] * lax.axis_size(('row', 'col'))),...]
    all_to_all x0 -> x1, waiting for transfers between devices: none -> 11.3 us  [precondition(): lax.all_to_all(jnp.stack([coefficients] * lax.axis_size(('row', 'col'))),...]
  transfers between devices with their start and end apart: 12 -> 13, of which waited for: 0 -> 1; matrix products, arithmetic and copies ran while one was open for 7% -> 10% of each run, Pallas kernels for 0% -> 0%
where the time goes in v1:
time: 617 us; the launch traced here: 611 us
  blocking collectives  444 us (72%)
  matrix products  57.5 us (9%)
  starting transfers between devices  45 us (7%)
  other arithmetic  29.2 us (5%)
  local copies, waits for them, and re-layouts  22.8 us (4%)
  waiting for transfers between devices  11.3 us (2%)
    psum x3, blocking collectives, pair_totals(): lax.psum((jnp.sum(first_field * second_field, axis=1), jnp.sum(third_fiel...  230 us
    psum x2, blocking collectives, shards(): cross_sum = lax.psum(jnp.sum(correction * image, axis=1), ('row', 'col'))  145 us
    all_to_all x3, blocking collectives, precondition(): lax.all_to_all(jnp.stack([coefficients] * lax.axis_size(('row', 'col'))),...  68 us
    dot_general x6, matrix products, sparse_forward(): product = jnp.einsum('lbkw,bkwv->lbv', picked, tile_set, precision=PRECISE)  23.5 us
    dot_general x6, matrix products, sparse_backward(): product = jnp.einsum('lbv,bkwv->lbkw', pieces, tile_set, precision=PRECISE)  21.4 us
    ppermute x6, starting transfers between devices, with_halo(): lax.ppermute(tail, axis, [(i, (i + 1) % count) for i in range(ends)])  18.7 us
    all_to_all x1, starting transfers between devices, precondition(): lax.all_to_all(jnp.stack([coefficients] * lax.axis_size(('row', 'col'))),...  15.6 us
  transfers between devices with their start and end apart: 13, of which 1 were waited for; matrix products, arithmetic and copies ran while one was open for 10% of the time, Pallas kernels for 0%

profile of v1, /device:TPU:1, one launch (start us, length us, event | category | flops | bytes accessed | tf_op | source)
XLA Modules:
  0.0 611.5 jit_solution(11242831021035833095)
XLA Ops:
  0.6 1.3 fusion.36
  2.1 1.1 reshape.361
  3.3 15.6 %all-to-all-start = ((f32[256,1,256]{2,1,0:T(1,128)}), f32[256,1,256]{2,1,0:T(1,128)S(1)}, u32[]{:S(2)}, u32[]{:S(2)}) async-start(f32[256,1,256]{2,1,0:T(1,128)} %reshape.361), calls=%async_computation | async-start | bytes 524288 | tf_op jit(solution)/shard_map/all_to_all | solution.py:99
  23.6 11.3 %all-to-all-done = f32[256,1,256]{2,1,0:T(1,128)S(1)} async-done(((f32[256,1,256]{2,1,0:T(1,128)}), f32[256,1,256]{2,1,0:T(1,128)S(1)}, u32[]{:S(2)}, u32[]{:S(2)}) %all-to-all-start) | async-done | bytes 262176 | tf_op jit(solution)/shard_map/all_to_all | solution.py:99
  35.4 1.3 reduce
  40.5 1.3 collective-permute-start
  41.9 1.3 collective-permute-start.1
  43.2 4.2 collective-permute-start.2
  47.5 2.2 collective-permute-start.3
  50.5 3.8 convolution_bitcast_fusion.17
  55.2 4.0 convolution_bitcast_fusion.16
  59.2 3.6 convolution_bitcast_fusion.5
  63.2 3.6 convolution_bitcast_fusion.4
  68.0 4.2 scatter_custom_fusion
  72.7 76.3 %all-reduce.2 = (f32[8]{0:T(128)S(1)}, f32[8]{0:T(128)S(1)}) all-reduce(f32[8]{0:T(128)S(1)} %get-tuple-element.10, f32[8]{0:T(128)S(1)} %get-tuple-element.9), channel_id=1, replica_groups=mesh['row'=16,'col'=16] {'row','col'}, use_global_device_ids=true, to_apply=%region_1.2 | all-reduce | flops 16 | bytes 128 | tf_op jit(solution)/shard_map/psum | solution.py:53
  151.0 22.4 %all_to_all.20 = f32[256,1,256]{2,1,0:T(1,128)S(1)} all-to-all(f32[256,1,256]{2,1,0:T(1,128)S(1)} %reshape.363), channel_id=1, replica_groups=mesh['row'=16,'col'=16] {'row','col'}, dimensions={0} | all-to-all | bytes 524288 | tf_op jit(solution)/shard_map/all_to_all | solution.py:99
  173.3 1.3 reduce.1
  176.5 1.2 multiply_reduce_fusion.5
  177.7 72.7 %psum.58 = f32[8]{0:T(128)S(1)} all-reduce(f32[8]{0:T(128)S(1)} %get-tuple-element.31), channel_id=1, replica_groups=mesh['row'=16,'col'=16] {'row','col'}, use_global_device_ids=true, to_apply=%region_6.9 | all-reduce | flops 8 | bytes 64 | tf_op jit(solution)/shard_map/psum | solution.py:121
  251.5 1.0 gather_fusion.5
  253.3 2.2 collective-permute-start.4
  255.6 1.3 collective-permute-start.5
  257.0 4.5 collective-permute-start.6
  261.6 2.1 collective-permute-start.7
  265.2 3.8 convolution_bitcast_fusion.15
  270.0 4.0 convolution_bitcast_fusion.14
  274.0 3.6 convolution_bitcast_fusion.3
  278.0 3.6 convolution_bitcast_fusion.2
  282.8 4.0 scatter_custom_fusion.1
  287.3 77.0 %all-reduce.1 = (f32[8]{0:T(128)S(1)}, f32[8]{0:T(128)S(1)}) all-reduce(f32[8]{0:T(128)S(1)} %get-tuple-element.8, f32[8]{0:T(128)S(1)} %get-tuple-element.7), channel_id=1, replica_groups=mesh['row'=16,'col'=16] {'row','col'}, use_global_device_ids=true, to_apply=%region_8.11 | all-reduce | flops 16 | bytes 128 | tf_op jit(solution)/shard_map/psum | solution.py:53
  365.5 1.1 fusion.40
  367.2 22.8 %all_to_all.21 = f32[256,1,256]{2,1,0:T(1,128)S(1)} all-to-all(f32[256,1,256]{2,1,0:T(1,128)S(1)} %reshape.365), channel_id=1, replica_groups=mesh['row'=16,'col'=16] {'row','col'}, dimensions={0} | all-to-all | bytes 524288 | tf_op jit(solution)/shard_map/all_to_all | solution.py:99
  390.0 1.3 reduce.2
  393.2 1.2 multiply_reduce_fusion.2
  394.4 72.7 %psum.61 = f32[8]{0:T(128)S(1)} all-reduce(f32[8]{0:T(128)S(1)} %get-tuple-element.33), channel_id=1, replica_groups=mesh['row'=16,'col'=16] {'row','col'}, use_global_device_ids=true, to_apply=%region_13.16 | all-reduce | flops 8 | bytes 64 | tf_op jit(solution)/shard_map/psum | solution.py:121
  470.1 4.2 collective-permute-start.10
  474.4 1.9 collective-permute-start.11
  476.3 2.2 collective-permute-start.8
  478.6 1.7 collective-permute-start.9
  481.9 3.8 convolution_bitcast_fusion.13
  486.7 4.0 convolution_bitcast_fusion.12
  490.7 3.6 convolution_bitcast_fusion.1
  494.7 3.6 convolution_bitcast_fusion
  499.4 4.0 scatter_custom_fusion.2
  504.8 77.2 %all-reduce = (f32[8]{0:T(128)S(1)}, f32[8]{0:T(128)S(1)}) all-reduce(f32[8]{0:T(128)S(1)} %get-tuple-element.6, f32[8]{0:T(128)S(1)} %get-tuple-element.5), channel_id=1, replica_groups=mesh['row'=16,'col'=16] {'row','col'}, use_global_device_ids=true, to_apply=%region_15.18 | all-reduce | flops 16 | bytes 128 | tf_op jit(solution)/shard_map/psum | solution.py:53
  582.0 1.6 multiply_subtract_fusion
  584.4 22.8 %all_to_all.22 = f32[256,1,256]{2,1,0:T(1,128)S(1)} all-to-all(f32[256,1,256]{2,1,0:T(1,128)S(1)} %reshape.367), channel_id=1, replica_groups=mesh['row'=16,'col'=16] {'row','col'}, dimensions={0} | all-to-all | bytes 524288 | tf_op jit(solution)/shard_map/all_to_all | solution.py:99
  607.2 1.3 reduce.3
  (187 shorter events, 38.5 us)
Async XLA Ops:
  0.6 37.1 %copy-start = (f32[32,8192]{1,0:T(8,128)S(1)}, f32[32,8192]{1,0:T(8,128)}, u32[]{:S(2)}) copy-start(f32[32,8192]{1,0:T(8,128)} %param.19) | copy-start | bytes 3145732
  2.1 36.5 %copy-start.7 = (f32[32,2048]{1,0:T(8,128)S(1)}, f32[32,2048]{1,0:T(8,128)}, u32[]{:S(2)}) copy-start(f32[32,2048]{1,0:T(8,128)} %param.18) | copy-start | bytes 786436
  2.1 36.5 %copy-start.8 = (f32[8,2048]{1,0:T(8,128)S(1)}, f32[8,2048]{1,0:T(8,128)}, u32[]{:S(2)}) copy-start(f32[8,2048]{1,0:T(8,128)} %param.13) | copy-start | bytes 196612
  3.3 31.6 %all-to-all-start = ((f32[256,1,256]{2,1,0:T(1,128)}), f32[256,1,256]{2,1,0:T(1,128)S(1)}, u32[]{:S(2)}, u32[]{:S(2)}) async-start(f32[256,1,256]{2,1,0:T(1,128)} %reshape.361), calls=%async_computation | async-start | bytes 524288 | tf_op jit(solution)/shard_map/all_to_all | solution.py:99
  20.3 47.4 %copy-start.14 = (pred[512]{0:T(512)(128)(4,1)}, pred[512]{0:T(512)(128)(4,1)S(1)}, u32[]{:S(2)}) copy-start(pred[512]{0:T(512)(128)(4,1)S(1)} %compare_and_fusion) | copy-start | bytes 1540
  21.2 29.2 %copy-start.22 = (pred[64]{0:T(512)(128)(4,1)}, pred[64]{0:T(512)(128)(4,1)S(1)}, u32[]{:S(2)}) copy-start(pred[64]{0:T(512)(128)(4,1)S(1)} %compare_and_fusion.2) | copy-start | bytes 196
  22.1 33.0 %copy-start.19 = (pred[64]{0:T(512)(128)(4,1)}, pred[64]{0:T(512)(128)(4,1)S(1)}, u32[]{:S(2)}) copy-start(pred[64]{0:T(512)(128)(4,1)S(1)} %compare_and_fusion.1) | copy-start | bytes 196
  22.1 27.6 %copy-start.18 = (s32[1024]{0:T(1024)}, s32[1024]{0:T(1024)S(1)}, u32[]{:S(2)}) copy-start(s32[1024]{0:T(1024)S(1)} %pad_clamp_fusion.2) | copy-start | bytes 12292
  22.1 32.3 %copy-start.17 = (s32[1024]{0:T(1024)}, s32[1024]{0:T(1024)S(1)}, u32[]{:S(2)}) copy-start(s32[1024]{0:T(1024)S(1)} %pad_clamp_fusion.1) | copy-start | bytes 12292
  23.6 44.4 %copy-start.23 = (s32[512,1]{0,1:T(1,128)}, s32[512,1]{0,1:T(1,128)S(1)}, u32[]{:S(2)}) copy-start(s32[512,1]{0,1:T(1,128)S(1)} %compare_select_fusion) | copy-start | bytes 6148
  40.5 27.1 %collective-permute-start = (f32[8,1,128]{2,0,1:T(8,128)S(1)}, f32[8,1,128]{2,0,1:T(8,128)S(1)}, u32[]{:S(2)}, u32[]{:S(2)}) collective-permute-start(f32[8,1,128]{2,0,1:T(8,128)S(1)} %copy.114), channel_id=1, source_target_pairs={{0,16},{16,32},{32,48},{48,64},{64,80},{80,96},{96,112},{112,128},... | collective-permute-start | bytes 12296 | tf_op jit(solution)/shard_map/ppermute | solution.py:18
  41.9 25.7 %collective-permute-start.1 = (f32[8,1,128]{2,0,1:T(8,128)S(1)}, f32[8,1,128]{2,0,1:T(8,128)S(1)}, u32[]{:S(2)}, u32[]{:S(2)}) collective-permute-start(f32[8,1,128]{2,0,1:T(8,128)S(1)} %copy.115), channel_id=1, source_target_pairs={{16,0},{32,16},{48,32},{64,48},{80,64},{96,80},{112,96},{128,112},... | collective-permute-start | bytes 12296 | tf_op jit(solution)/shard_map/ppermute | solution.py:20
  43.2 24.4 %collective-permute-start.2 = (f32[8,1,128]{2,0,1:T(8,128)S(1)}, f32[8,1,128]{2,0,1:T(8,128)S(1)}, u32[]{:S(2)}, u32[]{:S(2)}) collective-permute-start(f32[8,1,128]{2,0,1:T(8,128)S(1)} %copy.116), channel_id=1, source_target_pairs={{0,1},{1,2},{2,3},{3,4},{4,5},{5,6},{6,7},{7,8},{8,9},{9,10},{10,1... | collective-permute-start | bytes 12296 | tf_op jit(solution)/shard_map/ppermute | solution.py:18
  47.5 20.1 %collective-permute-start.3 = (f32[8,1,128]{2,0,1:T(8,128)S(1)}, f32[8,1,128]{2,0,1:T(8,128)S(1)}, u32[]{:S(2)}, u32[]{:S(2)}) collective-permute-start(f32[8,1,128]{2,0,1:T(8,128)S(1)} %copy.117), channel_id=1, source_target_pairs={{1,0},{2,1},{3,2},{4,3},{5,4},{6,5},{7,6},{8,7},{9,8},{10,9},{11,1... | collective-permute-start | bytes 12296 | tf_op jit(solution)/shard_map/ppermute | solution.py:20
  55.0 4.2 copy-start.1
  55.2 7.6 %copy-start.12 = (s32[16,4]{0,1:T(4,128)S(1)}, s32[16,4]{0,1:T(4,128)}, u32[]{:S(2)}) copy-start(s32[16,4]{0,1:T(4,128)} %param.17) | copy-start | bytes 772
  55.2 8.0 %copy-start.4 = (f32[8192,128]{1,0:T(8,128)S(1)}, f32[8192,128]{1,0:T(8,128)}, u32[]{:S(2)}) copy-start(f32[8192,128]{1,0:T(8,128)} %param.14) | copy-start | bytes 12582916
  59.2 7.6 %copy-start.13 = (s32[16,4]{0,1:T(4,128)S(1)}, s32[16,4]{0,1:T(4,128)}, u32[]{:S(2)}) copy-start(s32[16,4]{0,1:T(4,128)} %param.15) | copy-start | bytes 772
  72.5 77.8 %copy-start.10 = (f32[8,2048]{1,0:T(8,128)}, f32[8,2048]{1,0:T(8,128)S(1)}, u32[]{:S(2)}) copy-start(f32[8,2048]{1,0:T(8,128)S(1)} %copy.59) | copy-start | bytes 196612
  149.0 0.5 copy-start.29
  149.5 0.5 copy-start.24
  251.2 18.7 %copy-start.20 = (pred[64]{0:T(512)(128)(4,1)S(1)}, pred[64]{0:T(512)(128)(4,1)}, u32[]{:S(2)}) copy-start(pred[64]{0:T(512)(128)(4,1)} %copy-done.19) | copy-start | bytes 196
  253.3 29.0 %collective-permute-start.4 = (f32[8,1,128]{2,0,1:T(8,128)S(1)}, f32[8,1,128]{2,0,1:T(8,128)S(1)}, u32[]{:S(2)}, u32[]{:S(2)}) collective-permute-start(f32[8,1,128]{2,0,1:T(8,128)S(1)} %copy.118), channel_id=1, source_target_pairs={{0,16},{16,32},{32,48},{48,64},{64,80},{80,96},{96,112},{112,128},... | collective-permute-start | bytes 12296 | tf_op jit(solution)/shard_map/ppermute | solution.py:18
  255.6 26.8 %collective-permute-start.5 = (f32[8,1,128]{2,0,1:T(8,128)S(1)}, f32[8,1,128]{2,0,1:T(8,128)S(1)}, u32[]{:S(2)}, u32[]{:S(2)}) collective-permute-start(f32[8,1,128]{2,0,1:T(8,128)S(1)} %copy.119), channel_id=1, source_target_pairs={{16,0},{32,16},{48,32},{64,48},{80,64},{96,80},{112,96},{128,112},... | collective-permute-start | bytes 12296 | tf_op jit(solution)/shard_map/ppermute | solution.py:20
  257.0 25.4 %collective-permute-start.6 = (f32[8,1,128]{2,0,1:T(8,128)S(1)}, f32[8,1,128]{2,0,1:T(8,128)S(1)}, u32[]{:S(2)}, u32[]{:S(2)}) collective-permute-start(f32[8,1,128]{2,0,1:T(8,128)S(1)} %copy.120), channel_id=1, source_target_pairs={{0,1},{1,2},{2,3},{3,4},{4,5},{5,6},{6,7},{7,8},{8,9},{9,10},{10,1... | collective-permute-start | bytes 12296 | tf_op jit(solution)/shard_map/ppermute | solution.py:18
  261.6 20.8 %collective-permute-start.7 = (f32[8,1,128]{2,0,1:T(8,128)S(1)}, f32[8,1,128]{2,0,1:T(8,128)S(1)}, u32[]{:S(2)}, u32[]{:S(2)}) collective-permute-start(f32[8,1,128]{2,0,1:T(8,128)S(1)} %copy.121), channel_id=1, source_target_pairs={{1,0},{2,1},{3,2},{4,3},{5,4},{6,5},{7,6},{8,7},{9,8},{10,9},{11,1... | collective-permute-start | bytes 12296 | tf_op jit(solution)/shard_map/ppermute | solution.py:20
  269.9 4.2 copy-start.2
  270.0 8.0 %copy-start.5 = (f32[8192,128]{1,0:T(8,128)S(1)}, f32[8192,128]{1,0:T(8,128)}, u32[]{:S(2)}) copy-start(f32[8192,128]{1,0:T(8,128)} %param.14) | copy-start | bytes 12582916
  277.6 4.9 copy-start.15
  287.1 79.5 %copy-start.9 = (f32[8,2048]{1,0:T(8,128)}, f32[8,2048]{1,0:T(8,128)S(1)}, u32[]{:S(2)}) copy-start(f32[8,2048]{1,0:T(8,128)S(1)} %copy.73) | copy-start | bytes 196612
  364.3 2.4 copy-start.28
  364.3 0.5 copy-start.26
  467.9 18.6 %copy-start.21 = (pred[64]{0:T(512)(128)(4,1)S(1)}, pred[64]{0:T(512)(128)(4,1)}, u32[]{:S(2)}) copy-start(pred[64]{0:T(512)(128)(4,1)} %copy-done.19) | copy-start | bytes 196
  470.1 29.0 %collective-permute-start.10 = (f32[8,1,128]{2,0,1:T(8,128)S(1)}, f32[8,1,128]{2,0,1:T(8,128)S(1)}, u32[]{:S(2)}, u32[]{:S(2)}) collective-permute-start(f32[8,1,128]{2,0,1:T(8,128)S(1)} %copy.124), channel_id=1, source_target_pairs={{0,1},{1,2},{2,3},{3,4},{4,5},{5,6},{6,7},{7,8},{8,9},{9,10},{10,1... | collective-permute-start | bytes 12296 | tf_op jit(solution)/shard_map/ppermute | solution.py:18
  474.4 24.7 %collective-permute-start.11 = (f32[8,1,128]{2,0,1:T(8,128)S(1)}, f32[8,1,128]{2,0,1:T(8,128)S(1)}, u32[]{:S(2)}, u32[]{:S(2)}) collective-permute-start(f32[8,1,128]{2,0,1:T(8,128)S(1)} %copy.125), channel_id=1, source_target_pairs={{1,0},{2,1},{3,2},{4,3},{5,4},{6,5},{7,6},{8,7},{9,8},{10,9},{11,1... | collective-permute-start | bytes 12296 | tf_op jit(solution)/shard_map/ppermute | solution.py:20
  476.3 22.7 %collective-permute-start.8 = (f32[8,1,128]{2,0,1:T(8,128)S(1)}, f32[8,1,128]{2,0,1:T(8,128)S(1)}, u32[]{:S(2)}, u32[]{:S(2)}) collective-permute-start(f32[8,1,128]{2,0,1:T(8,128)S(1)} %copy.122), channel_id=1, source_target_pairs={{0,16},{16,32},{32,48},{48,64},{64,80},{80,96},{96,112},{112,128},... | collective-permute-start | bytes 12296 | tf_op jit(solution)/shard_map/ppermute | solution.py:18
  478.6 20.5 %collective-permute-start.9 = (f32[8,1,128]{2,0,1:T(8,128)S(1)}, f32[8,1,128]{2,0,1:T(8,128)S(1)}, u32[]{:S(2)}, u32[]{:S(2)}) collective-permute-start(f32[8,1,128]{2,0,1:T(8,128)S(1)} %copy.123), channel_id=1, source_target_pairs={{16,0},{32,16},{48,32},{64,48},{80,64},{96,80},{112,96},{128,112},... | collective-permute-start | bytes 12296 | tf_op jit(solution)/shard_map/ppermute | solution.py:20
  486.5 4.2 copy-start.3
  486.7 8.0 %copy-start.6 = (f32[8192,128]{1,0:T(8,128)S(1)}, f32[8192,128]{1,0:T(8,128)}, u32[]{:S(2)}) copy-start(f32[8192,128]{1,0:T(8,128)} %param.14) | copy-start | bytes 12582916
  494.3 5.0 copy-start.16
  494.7 87.3 %copy-start.25 = (f32[8]{0:T(128)S(1)}, f32[8]{0:T(128)}, u32[]{:S(2)}) copy-start(f32[8]{0:T(128)} %copy-done.24) | copy-start | bytes 100
  494.7 87.3 %copy-start.27 = (f32[8]{0:T(128)S(1)}, f32[8]{0:T(128)}, u32[]{:S(2)}) copy-start(f32[8]{0:T(128)} %copy-done.26) | copy-start | bytes 100
  583.5 26.9 %copy-start.11 = (f32[8,2048]{1,0:T(8,128)}, f32[8,2048]{1,0:T(8,128)S(1)}, u32[]{:S(2)}) copy-start(f32[8,2048]{1,0:T(8,128)S(1)} %get-tuple-element.29) | copy-start | bytes 196612
